TPU v7x, 32 devices: a whole 2x2x4 slice. The times are simulated.
32 devices in a mesh: ctx: 16 (over z, y, core), ch: 2 (over x).
Axes of the slice: x: 2, y: 2, z: 4, core: 2. Of those that a mesh axis runs over, the one named last changes fastest.
Arguments:
- tokens: bfloat16 [4096, 4096], P('ctx', 'ch'), may hold values from -6 to 6
- w_in: bfloat16 [4096, 3, 4096], P('ctx', None, 'ch'), may hold values from -0.09375 to 0.09375
- taps: float32 [3, 3, 4096], P(None, None, 'ch'), may hold values from -2 to 2
- modes_gain: float32 [16, 4096], P(None, 'ch'), may hold values from -1.5 to 1.5
- decay: float32 [16, 4096], P(None, 'ch'), may hold values from 0.3 to 300
- skip: float32 [4096], P('ch'), may hold values from -4 to 4
Outputs:
- mixed: bfloat16 [4096, 4096], P('ctx', 'ch')
All inputs are finite; a program needn't handle non-finite values.
Results may differ from a plain program's by a relative error of at most 0.0075.
Values may be sent and summed in bfloat16 or wider, within the bound.
A program may use at most 128 MiB of HBM per device.

v0:
```python
import functools

import jax
import jax.numpy as jnp
from jax import lax
from jax.experimental import pallas as pl
from jax.experimental.pallas import tpu as pltpu
from jax.sharding import PartitionSpec as P

SEGS = 8
LANES = 128


def flip(index, bits):
    out, bit = index, 1
    while bit <= bits:
        if bits & bit:
            out = out + bit - 2 * bit * ((index // bit) % 2)
        bit *= 2
    return out


def flip_traced(index, bits, count):
    out, bit = index, 1
    while bit < count:
        out = out + ((bits // bit) % 2) * (bit - 2 * bit * ((index // bit) % 2))
        bit *= 2
    return out


def piece_order(i, count):
    quarter = count // 4
    j = jnp.maximum(i - quarter, 0)
    turn = j % 3
    later = quarter + quarter * turn + j // 3
    return jnp.where(i < quarter, i, later)


def kernel(
    n_ctx, n_ch, groups,
    tokens, w_send, all_taps, all_gains, all_decay, all_skip, out,
    taps, gains, rates, skip, tok, w_recv, acc, prod, gate, state, ends, carry, sent, halo, halo_out,
    tok_ssem, tok_rsem, w_ssem, w_rsem, out_ssem, out_rsem, st_ssem, st_rsem, halo_sems, local_sems, own_sems,
):
    rows, width = tokens.shape
    wide = w_send.shape[2] // groups
    teams = n_ctx // groups
    span = groups * rows
    seg = span // SEGS
    lane_groups = wide // LANES
    ctx, ch = lax.axis_index("ctx"), lax.axis_index("ch")
    team, place = ctx // groups, ctx % groups

    hops = [("ctx", b) for b in reversed([2**i for i in range(1, groups.bit_length() - 1)])]
    hops += [("ch", b) for b in reversed([2**i for i in range(n_ch.bit_length() - 1)])]
    hops += [("ctx", 1)]
    depth = len(hops)

    def target(hop):
        axis, bit = hop
        return (flip(ctx, bit), ch) if axis == "ctx" else (ctx, flip(ch, bit))

    def slot_of(mask):
        cbits = sum(hops[i][1] for i in range(depth) if mask >> i & 1 and hops[i][0] == "ctx")
        hbits = sum(hops[i][1] for i in range(depth) if mask >> i & 1 and hops[i][0] == "ch")
        return flip(ch, hbits) * groups + flip(place, cbits)

    barrier = pltpu.get_barrier_semaphore()

    @pl.loop(1, n_ctx)
    def _(m):
        pl.semaphore_signal(barrier, inc=1, device_id=(flip_traced(ctx, m, n_ctx), ch), device_id_type=pl.DeviceIdType.MESH)

    ch_hops = [hop for hop in hops if hop[0] == "ch"]
    for hop in ch_hops:
        pl.semaphore_signal(barrier, inc=1, device_id=target(hop), device_id_type=pl.DeviceIdType.MESH)
    own_tok = pltpu.make_async_copy(tokens, tok.at[slot_of(0)], local_sems.at[0])
    own_tok.start()

    def w_columns(p, g):
        return w_send.at[:, :, pl.ds(pl.multiple_of(p * wide + g * LANES, LANES), LANES)]

    own_w = [pltpu.make_async_copy(w_columns(place, g), w_recv.at[g, 0], own_sems.at[0, g]) for g in range(lane_groups)]
    for copy in own_w:
        copy.start()
    own_lanes = pl.ds(pl.multiple_of(place * wide, LANES), wide)
    own_small = [
        pltpu.make_async_copy(all_taps.at[:, :, own_lanes], taps, local_sems.at[3]),
        pltpu.make_async_copy(all_gains.at[:, own_lanes], gains, local_sems.at[4]),
        pltpu.make_async_copy(all_decay.at[:, own_lanes], rates, local_sems.at[5]),
        pltpu.make_async_copy(all_skip.at[:, own_lanes], skip, local_sems.at[6]),
    ]
    for copy in own_small:
        copy.start()
    pl.semaphore_wait(barrier, n_ctx - 1 + len(ch_hops))

    def tok_copy(mask, i):
        src = tokens if mask == 0 else tok.at[slot_of(mask)]
        return pltpu.make_async_remote_copy(
            src_ref=src,
            dst_ref=tok.at[slot_of(mask)],
            send_sem=tok_ssem.at[mask, i],
            recv_sem=tok_rsem.at[mask | 1 << i],
            device_id=target(hops[i]),
            device_id_type=pl.DeviceIdType.MESH,
        )

    def arrived(mask):
        top = mask.bit_length() - 1
        pltpu.make_async_remote_copy(
            src_ref=tok.at[slot_of(mask)],
            dst_ref=tok.at[slot_of(mask)],
            send_sem=tok_ssem.at[0, top],
            recv_sem=tok_rsem.at[mask],
            device_id=target(hops[top]),
            device_id_type=pl.DeviceIdType.MESH,
        ).wait_recv()

    for i in range(depth):
        tok_copy(0, i).start()

    def w_copy(m, g):
        peer = flip_traced(ctx, m, n_ctx)
        return pltpu.make_async_remote_copy(
            src_ref=w_columns(peer % groups, g),
            dst_ref=w_recv.at[g, m],
            send_sem=w_ssem.at[g, m],
            recv_sem=w_rsem.at[g, m],
            device_id=(peer, ch),
            device_id_type=pl.DeviceIdType.MESH,
        )

    for g in range(lane_groups):
        @pl.loop(1, n_ctx)
        def _(i):
            w_copy(2 * piece_order(i // 2, n_ctx // 2) + i % 2, g).start()

    acc[...] = jnp.zeros_like(acc)
    masks = sorted(range(1, 2**depth), key=lambda m: (m.bit_length() if m.bit_length() == depth else 0, bin(m).count("1"), m))
    for mask in masks:
        arrived(mask)
        for i in range(mask.bit_length(), depth):
            tok_copy(mask, i).start()
    own_tok.wait()
    for copy in own_w + own_small:
        copy.wait()
    rates[...] = rates[...] / (rows * n_ctx)

    tall = groups
    header = SEGS

    modes = rates.shape[0]
    depth_rows = w_recv.shape[3]
    columns = [pl.ds(pl.multiple_of(place * wide + g * LANES, LANES), LANES) for g in range(lane_groups)]

    def project(g):
        @pl.loop(0, n_ctx // 2)
        def _(i):
            m = 2 * piece_order(i, n_ctx // 2)
            odd = ctx % 2

            @pl.when(i > 0)
            def _():
                w_copy(m, g).wait_recv()

            w_copy(m + 1, g).wait_recv()
            first = flip_traced(ctx - odd, m, n_ctx) * depth_rows
            half, column = first // width, first % width

            @pl.loop(0, groups // tall)
            def _(part):
                left = tok[pl.ds(half * groups + part * tall, tall), :, pl.ds(pl.multiple_of(column, LANES), 2 * depth_rows)]
                left = left.reshape(tall * rows, 2 * depth_rows)
                pair = (m + odd, m + 1 - odd)
                right = jnp.concatenate(
                    [jnp.concatenate([w_recv[g, p, j] for p in pair], axis=0) for j in range(3)], axis=1
                )
                where = pl.ds(pl.multiple_of(header + part * tall * rows, 8), tall * rows)
                acc[g, where, :] += jnp.dot(left, right, preferred_element_type=jnp.float32)

        @pl.loop(0, span // 64)
        def _(part):
            where = pl.ds(pl.multiple_of(header + part * 64, 8), 64)
            acc[g, where, :] = acc[g, where, :].astype(jnp.bfloat16).astype(jnp.float32)

    def halo_copy(g):
        return pltpu.make_async_remote_copy(
            src_ref=halo_out.at[g],
            dst_ref=halo.at[g],
            send_sem=halo_sems.at[g, 0],
            recv_sem=halo_sems.at[g, 1],
            device_id=((ctx + groups) % n_ctx, ch),
            device_id_type=pl.DeviceIdType.MESH,
        )

    def state_copy(k, g):
        return pltpu.make_async_remote_copy(
            src_ref=ends.at[g],
            dst_ref=carry.at[g, k],
            send_sem=st_ssem.at[g, k],
            recv_sem=st_rsem.at[g, k],
            device_id=((ctx + k * groups) % n_ctx, ch),
            device_id_type=pl.DeviceIdType.MESH,
        )

    def convolve(g):
        mine = slice(g * LANES, (g + 1) * LANES)
        halo_out[g] = acc[g, span : span + header, :]

        @pl.when(team < teams - 1)
        def _():
            halo_copy(g).start()

        acc[g, 0:header, :] = jnp.zeros((header, acc.shape[2]), jnp.float32)

        @pl.when(team > 0)
        def _():
            halo_copy(g).wait_recv()
            acc[g, 0:header, :] = halo[g]

        @pl.loop(0, SEGS)
        def _(s):
            base = pl.multiple_of(s * seg, 8)
            features = []
            for j in range(3):
                block = acc[g, pl.ds(base, seg + header), j * LANES : (j + 1) * LANES]
                total = taps[0, j : j + 1, mine] * block[header:]
                total += taps[1, j : j + 1, mine] * pltpu.roll(block, 1, 0)[header:]
                total += taps[2, j : j + 1, mine] * pltpu.roll(block, 2, 0)[header:]
                features.append(total)
            gate[g, pl.ds(s, seg, stride=SEGS), :] = features[0]
            prod[g, pl.ds(s, seg, stride=SEGS), :] = features[1] * features[2]

        def row(ref, m):
            return jnp.broadcast_to(ref[m : m + 1, mine], (SEGS, LANES))

        keep = [jnp.exp(-row(rates, m)) for m in range(modes)]

        def first_step(t, states):
            x = prod[g, pl.ds(pl.multiple_of(t * SEGS, SEGS), SEGS), :]
            return tuple(a * s + x for a, s in zip(keep, states))

        zeros = tuple(jnp.zeros((SEGS, LANES), jnp.float32) for _ in range(modes))
        last = lax.fori_loop(0, seg, first_step, zeros, unroll=2)
        for m in range(modes):
            state[g, m] = last[m]

        rate = rates[:, mine]
        jump = jnp.exp(-rate * float(seg))
        running = jnp.zeros_like(jump)
        for s in range(SEGS):
            ending = state[g, :, s, :]
            state[g, :, s, :] = running
            running = running * jump + ending
        ends[g] = running
        carry[g, 0] = jnp.zeros_like(jump)
        for k in range(1, teams):
            @pl.when(team + k < teams)
            def _():
                state_copy(k, g).start()
        for k in range(1, teams):
            @pl.when(team >= k)
            def _():
                state_copy(k, g).wait_recv()
                carry[g, 0] += carry[g, k] * jnp.exp(-rates[:, mine] * float((k - 1) * span))
        incoming = carry[g, 0]
        for s in range(SEGS):
            state[g, :, s, :] = state[g, :, s, :] + incoming * jnp.exp(-rate * float(s * seg))

        weight = [row(gains, m) * jnp.sqrt(2.0 * row(rates, m)) for m in range(modes)]
        direct = jnp.broadcast_to(skip[0:1, mine], (SEGS, LANES))

        def second_step(t, states):
            where = pl.ds(pl.multiple_of(t * SEGS, SEGS), SEGS)
            x = prod[g, where, :]
            states = tuple(a * s + x for a, s in zip(keep, states))
            terms = [w * s for w, s in zip(weight, states)] + [direct * x]
            while len(terms) > 1:
                terms = [a + b for a, b in zip(terms[::2], terms[1::2])] + ([terms[-1]] if len(terms) % 2 else [])
            gate[g, where, :] = gate[g, where, :] * terms[0]
            return states

        lax.fori_loop(0, seg, second_step, tuple(state[g, m] for m in range(modes)))

        @pl.loop(0, SEGS)
        def _(s):
            value = gate[g, pl.ds(s, seg, stride=SEGS), :]
            sent[g, pl.ds(pl.multiple_of(s * seg, 8), seg), :] = value.astype(sent.dtype)

    def out_rows(p, g):
        return sent.at[g, pl.ds(pl.multiple_of(p * rows, 16), rows), :]

    def out_copy(d, g):
        peer = flip_traced(place, d, groups)
        return pltpu.make_async_remote_copy(
            src_ref=out_rows(peer, g),
            dst_ref=out.at[:, columns[g]],
            send_sem=out_ssem.at[g, d],
            recv_sem=out_rsem.at[g, d],
            device_id=(team * groups + peer, ch),
            device_id_type=pl.DeviceIdType.MESH,
        )

    def out_arrival(d, g):
        peer = flip_traced(place, d, groups)
        spot = out.at[:, pl.ds(pl.multiple_of(peer * wide + g * LANES, LANES), LANES)]
        return pltpu.make_async_remote_copy(
            src_ref=spot,
            dst_ref=spot,
            send_sem=out_ssem.at[g, d],
            recv_sem=out_rsem.at[g, d],
            device_id=(team * groups + peer, ch),
            device_id_type=pl.DeviceIdType.MESH,
        )

    own_out = [pltpu.make_async_copy(out_rows(place, g), out.at[:, columns[g]], own_sems.at[1, g]) for g in range(lane_groups)]
    for g in range(lane_groups):
        project(g)
        convolve(g)

        @pl.loop(1, groups)
        def _(d):
            out_copy(groups - d, g).start()

        own_out[g].start()

    for i in range(depth):
        tok_copy(0, i).wait_send()
    for mask in masks:
        for i in range(mask.bit_length(), depth):
            tok_copy(mask, i).wait_send()

    for g in range(lane_groups):
        @pl.loop(1, n_ctx)
        def _(m):
            w_copy(m, g).wait_send()

        @pl.when(team < teams - 1)
        def _():
            halo_copy(g).wait_send()

        for k in range(1, teams):
            @pl.when(team + k < teams)
            def _():
                state_copy(k, g).wait_send()

        @pl.loop(1, groups)
        def _(d):
            out_arrival(d, g).wait_recv()
            out_copy(d, g).wait_send()

        own_out[g].wait()


def body(n_ctx, n_ch, tokens, w_in, taps, modes_gain, decay, skip):
    rows, width = tokens.shape
    e_rows, _, channels = w_in.shape
    modes = decay.shape[0]
    groups = min(n_ctx // 2, channels // LANES)
    teams = n_ctx // groups
    wide = channels // groups
    span = groups * rows
    parts = wide // LANES
    depth = (groups * n_ch).bit_length() - 1
    w_send = w_in.transpose(1, 0, 2)
    hbm = pl.BlockSpec(memory_space=pl.ANY)
    dma = pltpu.SemaphoreType.DMA
    f32 = jnp.float32
    return pl.pallas_call(
        functools.partial(kernel, n_ctx, n_ch, groups),
        out_shape=jax.ShapeDtypeStruct((rows, channels), jnp.bfloat16),
        in_specs=[hbm] * 6,
        out_specs=hbm,
        scratch_shapes=[
            pltpu.VMEM((3, 3, wide), f32),
            pltpu.VMEM((modes, wide), f32),
            pltpu.VMEM((modes, wide), f32),
            pltpu.VMEM((1, wide), f32),
            pltpu.VMEM((n_ch * groups, rows, width), tokens.dtype),
            pltpu.VMEM((parts, n_ctx, 3, e_rows, LANES), w_in.dtype),
            pltpu.VMEM((parts, SEGS + span, 3 * LANES), f32),
            pltpu.VMEM((parts, span, LANES), f32),
            pltpu.VMEM((parts, span, LANES), f32),
            pltpu.VMEM((parts, modes, SEGS, LANES), f32),
            pltpu.VMEM((parts, modes, LANES), f32),
            pltpu.VMEM((parts, teams, modes, LANES), f32),
            pltpu.VMEM((parts, span, LANES), jnp.bfloat16),
            pltpu.VMEM((parts, SEGS, 3 * LANES), f32),
            pltpu.VMEM((parts, SEGS, 3 * LANES), f32),
            dma((2**depth, depth)),
            dma((2**depth,)),
            dma((parts, n_ctx)),
            dma((parts, n_ctx)),
            dma((parts, groups)),
            dma((parts, groups)),
            dma((parts, teams)),
            dma((parts, teams)),
            dma((parts, 2)),
            dma((7,)),
            dma((2, parts)),
        ],
        compiler_params=pltpu.CompilerParams(
            collective_id=0, has_side_effects=True, vmem_limit_bytes=60 * 1024 * 1024
        ),
    )(tokens, w_send, taps, modes_gain, decay, skip[None])


def solution(mesh):
    in_specs = (
        P("ctx", "ch"),
        P("ctx", None, "ch"),
        P(None, None, "ch"),
        P(None, "ch"),
        P(None, "ch"),
        P("ch"),
    )
    step = functools.partial(body, mesh.shape["ctx"], mesh.shape["ch"])
    return jax.shard_map(step, mesh=mesh, in_specs=in_specs, out_specs=P("ctx", "ch"), check_vma=False)
```

profile of v0, /device:TPU:16, one launch (start us, length us, event | category | flops | bytes accessed | tf_op | source)
XLA Modules:
  0.0 176.9 jit_solution(1595010294927140119)
XLA Ops:
  0.0 174.6 %shard_map.64 = bf16[256,2048]{1,0:T(8,128)(2,1)} custom-call(bf16[256,2048]{1,0:T(8,128)(2,1)} %tokens.1, bf16[3,256,2048]{2,1,0:T(8,128)(2,1)} %bitcast.2, f32[3,3,2048]{2,1,0:T(4,128)} %all_taps.1, f32[16,2048]{1,0:T(8,128)} %all_gains.1, f32[16,2048]{1,0:T(8,128)} %all_decay.1, f32[1,2048]{1,0:T(1,128)} %bitcast.3), custom_call_target="tpu_custom_call" | custom-call | tf_op jit(solution)/shard_map/pallas_call | solution.py:369
  174.6 2.3 %copy.8 = bf16[256,2048]{1,0:T(8,128)(2,1)} copy(bf16[256,2048]{1,0:T(8,128)(2,1)} %shard_map.64) | data formatting | bytes 2097152
where the time goes:
time: 177 us
  Pallas kernels  175 us (99%)
  local copies, waits for them, and re-layouts  2.3 us (1%)
    pallas_call x1, Pallas kernels, body(): pl.pallas_call(functools.partial(kernel, n_ctx, n_ch, groups), out_shape=...  175 us

commit v1 on v0

v1 whole, which is shorter than its diff:
```python
import functools

import jax
import jax.numpy as jnp
from jax import lax
from jax.experimental import pallas as pl
from jax.experimental.pallas import tpu as pltpu
from jax.sharding import PartitionSpec as P

SEGS = 8
LANES = 128
MESH = pl.DeviceIdType.MESH


def flip(index, bits, count):
    out, bit = index, 1
    while bit < count:
        out = out + ((bits // bit) % 2) * (bit - 2 * bit * ((index // bit) % 2))
        bit *= 2
    return out


def piece_order(i, count):
    quarter = count // 4
    j = jnp.maximum(i - quarter, 0)
    later = quarter + quarter * (j % 3) + j // 3
    return jnp.where(i < quarter, i, later)


def kernel(
    n_ctx, n_ch, places,
    tokens, w_send, all_taps, all_gains, all_decay, all_skip, out,
    taps, gains, rates, skip, tok, w_recv, acc, prod, gate, state, ends, carry, sent, halo, halo_out,
    tok_ssem, tok_rsem, sib_ssem, w_ssem, w_rsem, f_ssem, f_rsem, out_ssem, out_rsem, st_ssem, st_rsem, halo_sems, local_sems, own_sems,
):
    rows, width = tokens.shape
    e_rows = w_send.shape[1]
    chips = n_ctx // 2
    teams = chips // places
    wide = w_send.shape[2] // places
    groups = wide // LANES
    lower = places // 2
    span = places * rows
    seg = span // SEGS
    header = SEGS
    modes = rates.shape[0]
    ctx, ch = lax.axis_index("ctx"), lax.axis_index("ch")
    chip, core = ctx // 2, ctx % 2
    team, place = chip // places, chip % places
    top, low = place // lower, place % lower
    other = 1 - core
    is_root = core == top
    sibling = (chip * 2 + other, ch)

    hops = [("low", b) for b in reversed([2**i for i in range(lower.bit_length() - 1)])]
    hops += [("ch", b) for b in reversed([2**i for i in range(n_ch.bit_length() - 1)])]
    depth = len(hops)

    def target(i):
        if i == depth:
            return (flip(chip, lower, chips) * 2 + core, ch)
        axis, bit = hops[i]
        return (flip(chip, bit, chips) * 2 + core, ch) if axis == "low" else (ctx, flip(ch, bit, n_ch))

    def slot_of(mask):
        lbits = sum(hops[i][1] for i in range(depth) if mask >> i & 1 and hops[i][0] == "low")
        hbits = sum(hops[i][1] for i in range(depth) if mask >> i & 1 and hops[i][0] == "ch")
        return flip(ch, hbits, n_ch) * lower + flip(low, lbits, lower)

    def unit(mask, c):
        return tok.at[slot_of(mask), pl.ds(pl.multiple_of(c * rows, 16), rows), :]

    barrier = pltpu.get_barrier_semaphore()

    @pl.loop(1, n_ctx)
    def _(m):
        pl.semaphore_signal(barrier, inc=1, device_id=(flip(ctx, m, n_ctx), ch), device_id_type=MESH)

    ch_hops = [i for i in range(depth) if hops[i][0] == "ch"]
    for i in ch_hops:
        pl.semaphore_signal(barrier, inc=1, device_id=target(i), device_id_type=MESH)

    own_tok = pltpu.make_async_copy(tokens, unit(0, core), local_sems.at[0])

    @pl.when(is_root)
    def _():
        own_tok.start()

    def w_columns(p, g):
        return w_send.at[:, :, pl.ds(pl.multiple_of(p * wide + g * LANES, LANES), LANES)]

    own_w = [pltpu.make_async_copy(w_columns(place, g), w_recv.at[g, 0, core], own_sems.at[0, g]) for g in range(groups)]
    for copy in own_w:
        copy.start()
    own_lanes = pl.ds(pl.multiple_of(place * wide, LANES), wide)
    own_small = [
        pltpu.make_async_copy(all_taps.at[:, :, own_lanes], taps, local_sems.at[1]),
        pltpu.make_async_copy(all_gains.at[:, own_lanes], gains, local_sems.at[2]),
        pltpu.make_async_copy(all_decay.at[:, own_lanes], rates, local_sems.at[3]),
        pltpu.make_async_copy(all_skip.at[:, own_lanes], skip, local_sems.at[4]),
    ]
    for copy in own_small:
        copy.start()
    pl.semaphore_wait(barrier, n_ctx - 1 + len(ch_hops))

    def tok_copy(mask, c, i, src=None):
        return pltpu.make_async_remote_copy(
            src_ref=unit(mask, c) if src is None else src,
            dst_ref=unit(mask, c),
            send_sem=tok_ssem.at[c, mask, i],
            recv_sem=tok_rsem.at[c, mask | (1 << i if i < depth else 0)],
            device_id=target(i),
            device_id_type=MESH,
        )

    sib_copy = pltpu.make_async_remote_copy(
        src_ref=tokens, dst_ref=unit(0, core), send_sem=sib_ssem, recv_sem=tok_rsem.at[core, 0], device_id=sibling, device_id_type=MESH
    )

    def tok_arrived(mask, c):
        pltpu.make_async_remote_copy(
            src_ref=unit(mask, c), dst_ref=unit(mask, c), send_sem=sib_ssem, recv_sem=tok_rsem.at[c, mask], device_id=sibling, device_id_type=MESH
        ).wait_recv()

    def relay(mask, c):
        for i in range(mask.bit_length(), depth):
            tok_copy(mask, c, i).start()

    def w_copy(m, g):
        peer = flip(chip, m, chips)
        return pltpu.make_async_remote_copy(
            src_ref=w_columns(peer % places, g),
            dst_ref=w_recv.at[g, m, core],
            send_sem=w_ssem.at[g, m],
            recv_sem=w_rsem.at[g, m],
            device_id=(peer * 2 + core, ch),
            device_id_type=MESH,
        )

    def f_copy(m, g, own=False):
        return pltpu.make_async_remote_copy(
            src_ref=w_columns(place, g) if own else w_recv.at[g, m, core],
            dst_ref=w_recv.at[g, m, core],
            send_sem=f_ssem.at[g, m],
            recv_sem=f_rsem.at[g, m],
            device_id=sibling,
            device_id_type=MESH,
        )

    def f_arrived(m, g):
        pltpu.make_async_remote_copy(
            src_ref=w_recv.at[g, m, other], dst_ref=w_recv.at[g, m, other], send_sem=f_ssem.at[g, m], recv_sem=f_rsem.at[g, m],
            device_id=sibling, device_id_type=MESH,
        ).wait_recv()

    @pl.when(is_root)
    def _():
        for i in [depth, *range(depth)]:
            tok_copy(0, core, i, tokens).start()

    @pl.when(jnp.logical_not(is_root))
    def _():
        sib_copy.start()

    f_copy(0, 0, True).start()

    @pl.when(is_root)
    def _():
        tok_arrived(0, other)
        for i in [depth, *range(depth)]:
            tok_copy(0, other, i).start()

    late = jnp.logical_and(core == 1, team < teams - 1) if groups > 1 and HOLD else None

    for g in range(groups):
        @pl.loop(1, chips)
        def _(i):
            m = piece_order(i, chips)
            if g > 0:
                skip_it = m == 1
                if g == groups - 1 and late is not None:
                    skip_it = jnp.logical_or(skip_it, jnp.logical_and(late, m >= places))

                @pl.when(jnp.logical_not(skip_it))
                def _():
                    w_copy(m, g).start()
            else:
                w_copy(m, g).start()

    acc[...] = jnp.zeros_like(acc)

    @pl.when(jnp.logical_not(is_root))
    def _():
        tok_arrived(0, core)
        relay(0, core)
        tok_arrived(0, other)
        relay(0, other)

    masks = sorted(range(1, 2**depth), key=lambda m: (m.bit_length(), bin(m).count("1"), m))
    n_low = lower.bit_length() - 1
    near = [mask for mask in masks if mask < 2**n_low]
    far = [mask for mask in masks if mask >= 2**n_low]

    def gather(which):
        for mask in which:
            for c in (core, other):
                tok_arrived(mask, c)
                relay(mask, c)

    gather(near)
    for g in range(1, groups):
        f_copy(0, g, True).start()
        w_copy(1, g).start()

    @pl.when(is_root)
    def _():
        own_tok.wait()
    for copy in own_small:
        copy.wait()
    rates[...] = rates[...] / (rows * n_ctx)

    per_half = chips // n_ch

    def near_first(i):
        return flip(ch, i // per_half, n_ch) * per_half + flip(chip % per_half, i % per_half, per_half)

    def in_order(i):
        return flip(chip, i, chips)

    def project(g, first, last, source):
        @pl.loop(first, last + 1)
        def _(i):
            @pl.when(i < last)
            def _():
                m = flip(chip, source(i), chips)

                @pl.when(m > 0)
                def _():
                    w_copy(m, g).wait_recv()
                    f_copy(m, g).start()

                @pl.when(m == 0)
                def _():
                    own_w[g].wait()

            @pl.when(i > first)
            def _():
                origin = source(i - 1)
                m = flip(chip, origin, chips)
                f_arrived(m, g)
                half, column = origin * 2 * e_rows // width, origin * 2 * e_rows % width
                left = tok[pl.ds(half * lower, lower), :, pl.ds(pl.multiple_of(column, LANES), 2 * e_rows)]
                left = left.reshape(span, 2 * e_rows)
                right = jnp.concatenate(
                    [jnp.concatenate([w_recv[g, m, c, j] for c in range(2)], axis=0) for j in range(3)], axis=1
                )
                acc[g, header:, :] += jnp.dot(left, right, preferred_element_type=jnp.float32)

    following = jnp.where(core == 0, sibling[0], (ctx + places * 2 - 1) % n_ctx)
    is_last = jnp.logical_and(core == 1, team == teams - 1)
    is_first = jnp.logical_and(core == 0, team == 0)

    def halo_copy(g):
        return pltpu.make_async_remote_copy(
            src_ref=halo_out.at[g],
            dst_ref=halo.at[g],
            send_sem=halo_sems.at[g, 0],
            recv_sem=halo_sems.at[g, 1],
            device_id=(following, ch),
            device_id_type=MESH,
        )

    def pair_copy(g):
        return pltpu.make_async_remote_copy(
            src_ref=ends.at[g, 0],
            dst_ref=carry.at[g, 0],
            send_sem=st_ssem.at[g, 0],
            recv_sem=st_rsem.at[g, 0],
            device_id=sibling,
            device_id_type=MESH,
        )

    def state_copy(g, k, c):
        return pltpu.make_async_remote_copy(
            src_ref=ends.at[g, 1],
            dst_ref=carry.at[g, k],
            send_sem=st_ssem.at[g, 2 * k - 1 + c],
            recv_sem=st_rsem.at[g, k],
            device_id=((chip + k * places) % chips * 2 + c, ch),
            device_id_type=MESH,
        )

    def row(ref, m, mine):
        return jnp.broadcast_to(ref[m : m + 1, mine], (SEGS, LANES))

    def lanes(g):
        return slice(g * LANES, (g + 1) * LANES)

    def first_half(g):
        mine = lanes(g)
        halo_out[g] = acc[g, span : span + header, :]

        @pl.when(jnp.logical_not(is_last))
        def _():
            halo_copy(g).start()

        @pl.when(is_first)
        def _():
            acc[g, 0:header, :] = jnp.zeros((header, acc.shape[2]), jnp.float32)

        @pl.when(jnp.logical_not(is_first))
        def _():
            halo_copy(g).wait_recv()
            acc[g, 0:header, :] = halo[g]

        @pl.loop(0, SEGS)
        def _(s):
            base = pl.multiple_of(s * seg, 8)
            features = []
            for j in range(3):
                block = acc[g, pl.ds(base, seg + header), j * LANES : (j + 1) * LANES]
                block = block.astype(jnp.bfloat16).astype(jnp.float32)
                total = taps[0, j : j + 1, mine] * block[header:]
                total += taps[1, j : j + 1, mine] * pltpu.roll(block, 1, 0)[header:]
                total += taps[2, j : j + 1, mine] * pltpu.roll(block, 2, 0)[header:]
                features.append(total)
            gate[g, pl.ds(s, seg, stride=SEGS), :] = features[0]
            prod[g, pl.ds(s, seg, stride=SEGS), :] = features[1] * features[2]

        keep = [jnp.exp(-row(rates, m, mine)) for m in range(modes)]

        def first_step(t, states):
            x = prod[g, pl.ds(pl.multiple_of(t * SEGS, SEGS), SEGS), :]
            return tuple(a * s + x for a, s in zip(keep, states))

        zeros = tuple(jnp.zeros((SEGS, LANES), jnp.float32) for _ in range(modes))
        last = lax.fori_loop(0, seg, first_step, zeros, unroll=2)
        for m in range(modes):
            state[g, m] = last[m]

        rate = rates[:, mine]
        jump = jnp.exp(-rate * float(seg))
        running = jnp.zeros_like(jump)
        for s in range(SEGS):
            ending = state[g, :, s, :]
            state[g, :, s, :] = running
            running = running * jump + ending
        ends[g, 0] = running

        @pl.when(core == 0)
        def _():
            pair_copy(g).start()

        @pl.when(core == 1)
        def _():
            pair_copy(g).wait_recv()
            ends[g, 1] = ends[g, 0] + carry[g, 0] * jnp.exp(-rate * float(span))
            for k in range(1, teams):
                @pl.when(team + k < teams)
                def _():
                    for c in range(2):
                        state_copy(g, k, c).start()

    def second_half(g):
        mine = lanes(g)
        rate = rates[:, mine]
        incoming = jnp.zeros_like(rate)
        ends[g, 2] = incoming
        for k in range(1, teams):
            @pl.when(team >= k)
            def _():
                state_copy(g, k, core).wait_recv()
                ends[g, 2] += carry[g, k] * jnp.exp(-rate * float((k - 1) * 2 * span))

        @pl.when(core == 1)
        def _():
            ends[g, 2] = ends[g, 2] * jnp.exp(-rate * float(span)) + carry[g, 0]

        incoming = ends[g, 2]
        for s in range(SEGS):
            state[g, :, s, :] = state[g, :, s, :] + incoming * jnp.exp(-rate * float(s * seg))

        keep = [jnp.exp(-row(rates, m, mine)) for m in range(modes)]
        weight = [row(gains, m, mine) * jnp.sqrt(2.0 * row(rates, m, mine)) for m in range(modes)]
        direct = jnp.broadcast_to(skip[0:1, mine], (SEGS, LANES))

        def second_step(t, states):
            where = pl.ds(pl.multiple_of(t * SEGS, SEGS), SEGS)
            x = prod[g, where, :]
            states = tuple(a * s + x for a, s in zip(keep, states))
            terms = [w * s for w, s in zip(weight, states)] + [direct * x]
            while len(terms) > 1:
                terms = [a + b for a, b in zip(terms[::2], terms[1::2])] + ([terms[-1]] if len(terms) % 2 else [])
            gate[g, where, :] = gate[g, where, :] * terms[0]
            return states

        lax.fori_loop(0, seg, second_step, tuple(state[g, m] for m in range(modes)))

        @pl.loop(0, SEGS)
        def _(s):
            value = gate[g, pl.ds(s, seg, stride=SEGS), :]
            sent[g, pl.ds(pl.multiple_of(s * seg, 8), seg), :] = value.astype(sent.dtype)

        @pl.when(is_root)
        def _():
            own_out(g).start()

        @pl.when(jnp.logical_not(is_root))
        def _():
            out_copy(0, g).start()

        @pl.loop(1, places)
        def _(d):
            out_copy(places - d, g).start()

    def columns(p, g):
        return out.at[:, pl.ds(pl.multiple_of(p * wide + g * LANES, LANES), LANES)]

    def out_rows(d, g):
        return sent.at[g, pl.ds(pl.multiple_of(d * rows, 16), rows), :]

    def own_out(g):
        return pltpu.make_async_copy(out_rows(low * 2 + core, g), columns(place, g), own_sems.at[1, g])

    def out_copy(o, g):
        d = flip(low * 2 + core, o, places)
        peer = team * places + core * lower + d // 2
        return pltpu.make_async_remote_copy(
            src_ref=out_rows(d, g),
            dst_ref=columns(place, g),
            send_sem=out_ssem.at[g, o],
            recv_sem=out_rsem.at[g, place],
            device_id=(peer * 2 + d % 2, ch),
            device_id_type=MESH,
        )

    def out_arrived(p, g):
        pltpu.make_async_remote_copy(
            src_ref=columns(p, g), dst_ref=columns(p, g), send_sem=out_ssem.at[g, 0], recv_sem=out_rsem.at[g, p],
            device_id=sibling, device_id_type=MESH,
        ).wait_recv()

    for g in range(groups - 1):
        project(g, 0, per_half, near_first)
    gather(far)
    for g in range(groups - 1):
        project(g, per_half, chips, near_first)
        first_half(g)
        if g > 0:
            second_half(g - 1)
    if groups > 1:
        if late is not None:
            @pl.when(late)
            def _():
                @pl.loop(places, chips)
                def _(i):
                    w_copy(i, groups - 1).start()

        project(groups - 1, 0, places, in_order)
        second_half(groups - 2)
        project(groups - 1, places, chips, in_order)
    else:
        project(0, 0, chips, in_order)
    first_half(groups - 1)
    second_half(groups - 1)

    @pl.when(is_root)
    def _():
        for c in (core, other):
            for i in range(depth + 1):
                tok_copy(0, c, i).wait_send()

    @pl.when(jnp.logical_not(is_root))
    def _():
        sib_copy.wait_send()
        for c in (core, other):
            for i in range(depth):
                tok_copy(0, c, i).wait_send()

    for mask in masks:
        for c in (core, other):
            for i in range(mask.bit_length(), depth):
                tok_copy(mask, c, i).wait_send()

    for g in range(groups):
        f_copy(0, g, True).wait_send()

        @pl.loop(1, chips)
        def _(m):
            w_copy(m, g).wait_send()
            f_copy(m, g).wait_send()

        @pl.when(jnp.logical_not(is_last))
        def _():
            halo_copy(g).wait_send()

        @pl.when(core == 0)
        def _():
            pair_copy(g).wait_send()

        for k in range(1, teams):
            @pl.when(jnp.logical_and(core == 1, team + k < teams))
            def _():
                for c in range(2):
                    state_copy(g, k, c).wait_send()

        @pl.when(is_root)
        def _():
            own_out(g).wait()

        @pl.when(jnp.logical_not(is_root))
        def _():
            out_copy(0, g).wait_send()

        @pl.loop(1, places)
        def _(d):
            out_copy(d, g).wait_send()

        @pl.loop(0, places)
        def _(p):
            @pl.when(jnp.logical_or(p != place, jnp.logical_not(is_root)))
            def _():
                out_arrived(p, g)


HOLD = True


def body(n_ctx, n_ch, tokens, w_in, taps, modes_gain, decay, skip):
    rows, width = tokens.shape
    e_rows, _, channels = w_in.shape
    modes = decay.shape[0]
    chips = n_ctx // 2
    places = min(chips // 2, channels // LANES)
    teams = chips // places
    wide = channels // places
    span = places * rows
    groups = wide // LANES
    lower = places // 2
    depth = (lower * n_ch).bit_length() - 1
    w_send = w_in.transpose(1, 0, 2)
    hbm = pl.BlockSpec(memory_space=pl.ANY)
    dma = pltpu.SemaphoreType.DMA
    f32 = jnp.float32
    return pl.pallas_call(
        functools.partial(kernel, n_ctx, n_ch, places),
        out_shape=jax.ShapeDtypeStruct((rows, channels), jnp.bfloat16),
        in_specs=[hbm] * 6,
        out_specs=hbm,
        scratch_shapes=[
            pltpu.VMEM((3, 3, wide), f32),
            pltpu.VMEM((modes, wide), f32),
            pltpu.VMEM((modes, wide), f32),
            pltpu.VMEM((1, wide), f32),
            pltpu.VMEM((n_ch * lower, 2 * rows, width), tokens.dtype),
            pltpu.VMEM((groups, chips, 2, 3, e_rows, LANES), w_in.dtype),
            pltpu.VMEM((groups, SEGS + span, 3 * LANES), f32),
            pltpu.VMEM((groups, span, LANES), f32),
            pltpu.VMEM((groups, span, LANES), f32),
            pltpu.VMEM((groups, modes, SEGS, LANES), f32),
            pltpu.VMEM((groups, 3, modes, LANES), f32),
            pltpu.VMEM((groups, teams, modes, LANES), f32),
            pltpu.VMEM((groups, span, LANES), jnp.bfloat16),
            pltpu.VMEM((groups, SEGS, 3 * LANES), f32),
            pltpu.VMEM((groups, SEGS, 3 * LANES), f32),
            dma((2, 2**depth, depth + 1)),
            dma((2, 2**depth)),
            dma,
            dma((groups, chips)),
            dma((groups, chips)),
            dma((groups, chips)),
            dma((groups, chips)),
            dma((groups, places)),
            dma((groups, places)),
            dma((groups, 2 * teams)),
            dma((groups, teams)),
            dma((groups, 2)),
            dma((5,)),
            dma((2, groups)),
        ],
        compiler_params=pltpu.CompilerParams(
            collective_id=0, has_side_effects=True, vmem_limit_bytes=48 * 1024 * 1024
        ),
    )(tokens, w_send, taps, modes_gain, decay, skip[None])


def solution(mesh):
    in_specs = (
        P("ctx", "ch"),
        P("ctx", None, "ch"),
        P(None, None, "ch"),
        P(None, "ch"),
        P(None, "ch"),
        P("ch"),
    )
    step = functools.partial(body, mesh.shape["ctx"], mesh.shape["ch"])
    return jax.shard_map(step, mesh=mesh, in_specs=in_specs, out_specs=P("ctx", "ch"), check_vma=False)
```

time: 177 us -> 184 us (1.040)
  local copies, waits for them, and re-layouts: 2.3 us -> 7.48 us
    unnamed x1 -> x13, local copies, waits for them, and re-layouts: 2.3 us -> 7.48 us
where the time goes in v1:
time: 184 us
  Pallas kernels  176 us (96%)
  local copies, waits for them, and re-layouts  7.48 us (4%)
    pallas_call x1, Pallas kernels, body(): pl.pallas_call(functools.partial(kernel, n_ctx, n_ch, places), out_shape=...  176 us
    unnamed x13, local copies, waits for them, and re-layouts  7.48 us

profile of v1, /device:TPU:16, one launch (start us, length us, event | category | flops | bytes accessed | tf_op | source)
XLA Modules:
  0.0 183.9 jit_solution(7595345463230210477)
XLA Ops:
  0.0 0.0 copy-start
  0.0 1.9 %copy-done = bf16[256,3,2048]{2,0,1:T(8,128)(2,1)S(1)} copy-done((bf16[256,3,2048]{2,0,1:T(8,128)(2,1)S(1)}, bf16[256,3,2048]{2,0,1:T(8,128)(2,1)}, u32[]{:S(2)}) %copy-start) | copy-done | bytes 3145752
  1.9 0.0 copy-start.1
  1.9 1.2 copy-done.1
  3.1 0.0 copy-start.2
  3.1 0.9 copy-done.2
  4.0 0.0 copy-start.3
  4.0 0.9 copy-done.3
  4.9 0.0 copy-start.4
  4.9 0.9 copy-done.4
  5.8 0.0 copy-start.5
  5.8 0.7 copy-done.5
  6.5 176.4 %shard_map.64 = bf16[256,2048]{1,0:T(8,128)(2,1)S(1)} custom-call(bf16[256,2048]{1,0:T(8,128)(2,1)S(1)} %copy-done.1, bf16[3,256,2048]{2,1,0:T(8,128)(2,1)S(1)} %bitcast.2, f32[3,3,2048]{2,1,0:T(4,128)S(1)} %copy-done.4, f32[16,2048]{1,0:T(8,128)S(1)} %copy-done.2, f32[16,2048]{1,0:T(8,128)S(1)} %copy-done.3, f32[1,2048]{1,0:T(1,128)S(1)} %bitcast.3), custom_call_target="tpu_custom_call" | custom-call | tf_op jit(solution)/shard_map/pallas_call | solution.py:545
  183.0 1.0 copy.8
Async XLA Ops:
  0.0 1.9 %copy-start = (bf16[256,3,2048]{2,0,1:T(8,128)(2,1)S(1)}, bf16[256,3,2048]{2,0,1:T(8,128)(2,1)}, u32[]{:S(2)}) copy-start(bf16[256,3,2048]{2,0,1:T(8,128)(2,1)} %param.7) | copy-start | bytes 9437188
  1.9 1.2 copy-start.1
  3.1 0.9 copy-start.2
  4.0 0.9 copy-start.3
  4.9 0.9 copy-start.4
  5.8 0.7 copy-start.5

commit v2 on v0

--- a/solution.py
+++ b/solution.py
@@ -9,6 +9,7 @@
 
 SEGS = 8
 LANES = 128
+HELD = 2
 
 
 def flip(index, bits):
@@ -130,58 +131,77 @@
             device_id_type=pl.DeviceIdType.MESH,
         )
 
-    for g in range(lane_groups):
-        @pl.loop(1, n_ctx)
+    waiting = team < teams - 1
+
+    def send(g, first, last):
+        @pl.loop(first, last)
         def _(i):
             w_copy(2 * piece_order(i // 2, n_ctx // 2) + i % 2, g).start()
 
+    for g in range(lane_groups - 1):
+        send(g, 1, n_ctx)
+    if lane_groups > 1:
+        send(lane_groups - 1, 1, n_ctx - HELD)
+
+        @pl.when(jnp.logical_not(waiting))
+        def _():
+            send(lane_groups - 1, n_ctx - HELD, n_ctx)
+    else:
+        send(0, 1, n_ctx)
+
     acc[...] = jnp.zeros_like(acc)
     masks = sorted(range(1, 2**depth), key=lambda m: (m.bit_length() if m.bit_length() == depth else 0, bin(m).count("1"), m))
-    for mask in masks:
-        arrived(mask)
-        for i in range(mask.bit_length(), depth):
-            tok_copy(mask, i).start()
+    crossing = sum(1 << i for i in range(depth) if hops[i][0] == "ch")
+
+    def gather(which):
+        for mask in which:
+            arrived(mask)
+            for i in range(mask.bit_length(), depth):
+                tok_copy(mask, i).start()
+
+    gather([mask for mask in masks if not mask & crossing])
     own_tok.wait()
     for copy in own_w + own_small:
         copy.wait()
     rates[...] = rates[...] / (rows * n_ctx)
 
-    tall = groups
     header = SEGS
 
     modes = rates.shape[0]
     depth_rows = w_recv.shape[3]
     columns = [pl.ds(pl.multiple_of(place * wide + g * LANES, LANES), LANES) for g in range(lane_groups)]
 
-    def project(g):
-        @pl.loop(0, n_ctx // 2)
+    chips = n_ctx // 2
+    per_half = chips // n_ch
+
+    def near_first(i):
+        home = ctx // 2
+        origin = flip_traced(ch, i // per_half, n_ch) * per_half + flip_traced(home % per_half, i % per_half, per_half)
+        return flip_traced(home, origin, chips)
+
+    def in_order(i):
+        return piece_order(i, chips)
+
+    def project(g, first, last, source):
+        @pl.loop(first, last)
         def _(i):
-            m = 2 * piece_order(i, n_ctx // 2)
+            m = 2 * source(i)
             odd = ctx % 2
 
-            @pl.when(i > 0)
+            @pl.when(m > 0)
             def _():
                 w_copy(m, g).wait_recv()
 
             w_copy(m + 1, g).wait_recv()
-            first = flip_traced(ctx - odd, m, n_ctx) * depth_rows
-            half, column = first // width, first % width
-
-            @pl.loop(0, groups // tall)
-            def _(part):
-                left = tok[pl.ds(half * groups + part * tall, tall), :, pl.ds(pl.multiple_of(column, LANES), 2 * depth_rows)]
-                left = left.reshape(tall * rows, 2 * depth_rows)
-                pair = (m + odd, m + 1 - odd)
-                right = jnp.concatenate(
-                    [jnp.concatenate([w_recv[g, p, j] for p in pair], axis=0) for j in range(3)], axis=1
-                )
-                where = pl.ds(pl.multiple_of(header + part * tall * rows, 8), tall * rows)
-                acc[g, where, :] += jnp.dot(left, right, preferred_element_type=jnp.float32)
-
-        @pl.loop(0, span // 64)
-        def _(part):
-            where = pl.ds(pl.multiple_of(header + part * 64, 8), 64)
-            acc[g, where, :] = acc[g, where, :].astype(jnp.bfloat16).astype(jnp.float32)
+            origin = flip_traced(ctx - odd, m, n_ctx) * depth_rows
+            half, column = origin // width, origin % width
+            left = tok[pl.ds(half * groups, groups), :, pl.ds(pl.multiple_of(column, LANES), 2 * depth_rows)]
+            left = left.reshape(span, 2 * depth_rows)
+            pair = (m + odd, m + 1 - odd)
+            right = jnp.concatenate(
+                [jnp.concatenate([w_recv[g, p, j] for p in pair], axis=0) for j in range(3)], axis=1
+            )
+            acc[g, header:, :] += jnp.dot(left, right, preferred_element_type=jnp.float32)
 
     def halo_copy(g):
         return pltpu.make_async_remote_copy(
@@ -203,27 +223,42 @@
             device_id_type=pl.DeviceIdType.MESH,
         )
 
-    def convolve(g):
-        mine = slice(g * LANES, (g + 1) * LANES)
+    def send_halo(g):
         halo_out[g] = acc[g, span : span + header, :]
 
         @pl.when(team < teams - 1)
         def _():
             halo_copy(g).start()
 
-        acc[g, 0:header, :] = jnp.zeros((header, acc.shape[2]), jnp.float32)
-
-        @pl.when(team > 0)
-        def _():
-            halo_copy(g).wait_recv()
-            acc[g, 0:header, :] = halo[g]
-
-        @pl.loop(0, SEGS)
-        def _(s):
+    def row(ref, m, mine):
+        return jnp.broadcast_to(ref[m : m + 1, mine], (SEGS, LANES))
+
+    def decays(mine):
+        return [jnp.exp(-row(rates, m, mine)) for m in range(modes)]
+
+    def first_half(g):
+        mine = slice(g * LANES, (g + 1) * LANES)
+
+        @pl.loop(1, SEGS + 1)
+        def _(turn):
+            s = turn % SEGS
+
+            @pl.when(s == 0)
+            def _():
+                @pl.when(team == 0)
+                def _():
+                    acc[g, 0:header, :] = jnp.zeros((header, acc.shape[2]), jnp.float32)
+
+                @pl.when(team > 0)
+                def _():
+                    halo_copy(g).wait_recv()
+                    acc[g, 0:header, :] = halo[g]
+
             base = pl.multiple_of(s * seg, 8)
             features = []
             for j in range(3):
                 block = acc[g, pl.ds(base, seg + header), j * LANES : (j + 1) * LANES]
+                block = block.astype(jnp.bfloat16).astype(jnp.float32)
                 total = taps[0, j : j + 1, mine] * block[header:]
                 total += taps[1, j : j + 1, mine] * pltpu.roll(block, 1, 0)[header:]
                 total += taps[2, j : j + 1, mine] * pltpu.roll(block, 2, 0)[header:]
@@ -231,17 +266,14 @@
             gate[g, pl.ds(s, seg, stride=SEGS), :] = features[0]
             prod[g, pl.ds(s, seg, stride=SEGS), :] = features[1] * features[2]
 
-        def row(ref, m):
-            return jnp.broadcast_to(ref[m : m + 1, mine], (SEGS, LANES))
-
-        keep = [jnp.exp(-row(rates, m)) for m in range(modes)]
+        keep = decays(mine)
 
         def first_step(t, states):
             x = prod[g, pl.ds(pl.multiple_of(t * SEGS, SEGS), SEGS), :]
             return tuple(a * s + x for a, s in zip(keep, states))
 
         zeros = tuple(jnp.zeros((SEGS, LANES), jnp.float32) for _ in range(modes))
-        last = lax.fori_loop(0, seg, first_step, zeros, unroll=2)
+        last = lax.fori_loop(0, seg, first_step, zeros, unroll=4)
         for m in range(modes):
             state[g, m] = last[m]
 
@@ -258,6 +290,10 @@
             @pl.when(team + k < teams)
             def _():
                 state_copy(k, g).start()
+
+    def second_half(g):
+        mine = slice(g * LANES, (g + 1) * LANES)
+        rate = rates[:, mine]
         for k in range(1, teams):
             @pl.when(team >= k)
             def _():
@@ -267,7 +303,8 @@
         for s in range(SEGS):
             state[g, :, s, :] = state[g, :, s, :] + incoming * jnp.exp(-rate * float(s * seg))
 
-        weight = [row(gains, m) * jnp.sqrt(2.0 * row(rates, m)) for m in range(modes)]
+        keep = decays(mine)
+        weight = [row(gains, m, mine) * jnp.sqrt(2.0 * row(rates, m, mine)) for m in range(modes)]
         direct = jnp.broadcast_to(skip[0:1, mine], (SEGS, LANES))
 
         def second_step(t, states):
@@ -280,7 +317,7 @@
             gate[g, where, :] = gate[g, where, :] * terms[0]
             return states
 
-        lax.fori_loop(0, seg, second_step, tuple(state[g, m] for m in range(modes)))
+        lax.fori_loop(0, seg, second_step, tuple(state[g, m] for m in range(modes)), unroll=4)
 
         @pl.loop(0, SEGS)
         def _(s):
@@ -314,15 +351,42 @@
         )
 
     own_out = [pltpu.make_async_copy(out_rows(place, g), out.at[:, columns[g]], own_sems.at[1, g]) for g in range(lane_groups)]
-    for g in range(lane_groups):
-        project(g)
-        convolve(g)
-
+    def give_out(g):
         @pl.loop(1, groups)
         def _(d):
             out_copy(groups - d, g).start()
 
         own_out[g].start()
+
+    tail = lane_groups - 1
+    far = [mask for mask in masks if mask & crossing]
+    if tail:
+        project(0, 0, per_half, near_first)
+    gather(far)
+    for g in range(tail):
+        project(g, per_half if g == 0 else 0, chips, near_first)
+        send_halo(g)
+        first_half(g)
+        if g == tail - 1:
+            @pl.when(waiting)
+            def _():
+                send(tail, n_ctx - HELD, n_ctx)
+
+        if g < tail - 1:
+            second_half(g)
+            give_out(g)
+    half_way = chips // 2
+    if tail:
+        project(tail, 0, half_way, in_order)
+        second_half(tail - 1)
+        give_out(tail - 1)
+        project(tail, half_way, chips, in_order)
+    else:
+        project(0, 0, chips, in_order)
+    send_halo(tail)
+    first_half(tail)
+    second_half(tail)
+    give_out(tail)
 
     for i in range(depth):
         tok_copy(0, i).wait_send()

time: 177 us -> 167 us (0.944)
  Pallas kernels: 175 us -> 164 us
    pallas_call x1, Pallas kernels: 175 us -> 164 us  [body(): pl.pallas_call(functools.partial(kernel, n_ctx, n_ch, groups), out_shape=...]
where the time goes in v2:
time: 167 us; the launch traced here: 166 us
  Pallas kernels  164 us (98%)
  local copies, waits for them, and re-layouts  2.3 us (1%)
    pallas_call x1, Pallas kernels, body(): pl.pallas_call(functools.partial(kernel, n_ctx, n_ch, groups), out_shape=...  164 us

profile of v2, /device:TPU:16, one launch (start us, length us, event | category | flops | bytes accessed | tf_op | source)
XLA Modules:
  0.0 166.1 jit_solution(13748941289947502336)
XLA Ops:
  0.0 163.8 %shard_map.64 = bf16[256,2048]{1,0:T(8,128)(2,1)} custom-call(bf16[256,2048]{1,0:T(8,128)(2,1)} %tokens.1, bf16[3,256,2048]{2,1,0:T(8,128)(2,1)} %bitcast.2, f32[3,3,2048]{2,1,0:T(4,128)} %all_taps.1, f32[16,2048]{1,0:T(8,128)} %all_gains.1, f32[16,2048]{1,0:T(8,128)} %all_decay.1, f32[1,2048]{1,0:T(1,128)} %bitcast.3), custom_call_target="tpu_custom_call" | custom-call | tf_op jit(solution)/shard_map/pallas_call | solution.py:433
  163.8 2.3 %copy.8 = bf16[256,2048]{1,0:T(8,128)(2,1)} copy(bf16[256,2048]{1,0:T(8,128)(2,1)} %shard_map.64) | data formatting | bytes 2097152

commit v3 on v2

--- a/solution.py
+++ b/solution.py
@@ -375,7 +375,7 @@
         if g < tail - 1:
             second_half(g)
             give_out(g)
-    half_way = chips // 2
+    half_way = 0
     if tail:
         project(tail, 0, half_way, in_order)
         second_half(tail - 1)

time: 167 us -> 164 us (0.982)
  Pallas kernels: 164 us -> 162 us
    pallas_call x1, Pallas kernels: 164 us -> 162 us  [body(): pl.pallas_call(functools.partial(kernel, n_ctx, n_ch, groups), out_shape=...]
where the time goes in v3:
time: 164 us
  Pallas kernels  162 us (99%)
  local copies, waits for them, and re-layouts  2.3 us (1%)
    pallas_call x1, Pallas kernels, body(): pl.pallas_call(functools.partial(kernel, n_ctx, n_ch, groups), out_shape=...  162 us

profile of v3, /device:TPU:16, one launch (start us, length us, event | category | flops | bytes accessed | tf_op | source)
XLA Modules:
  0.0 164.0 jit_solution(13616408835775663221)
XLA Ops:
  0.0 161.7 %shard_map.64 = bf16[256,2048]{1,0:T(8,128)(2,1)} custom-call(bf16[256,2048]{1,0:T(8,128)(2,1)} %tokens.1, bf16[3,256,2048]{2,1,0:T(8,128)(2,1)} %bitcast.2, f32[3,3,2048]{2,1,0:T(4,128)} %all_taps.1, f32[16,2048]{1,0:T(8,128)} %all_gains.1, f32[16,2048]{1,0:T(8,128)} %all_decay.1, f32[1,2048]{1,0:T(1,128)} %bitcast.3), custom_call_target="tpu_custom_call" | custom-call | tf_op jit(solution)/shard_map/pallas_call | solution.py:433
  161.7 2.3 %copy.8 = bf16[256,2048]{1,0:T(8,128)(2,1)} copy(bf16[256,2048]{1,0:T(8,128)(2,1)} %shard_map.64) | data formatting | bytes 2097152

commit v4 on v3

--- a/solution.py
+++ b/solution.py
@@ -10,6 +10,7 @@
 SEGS = 8
 LANES = 128
 HELD = 2
+PARTS = 2
 
 
 def flip(index, bits):
@@ -30,11 +31,8 @@
 
 
 def piece_order(i, count):
-    quarter = count // 4
-    j = jnp.maximum(i - quarter, 0)
-    turn = j % 3
-    later = quarter + quarter * turn + j // 3
-    return jnp.where(i < quarter, i, later)
+    half = count // 2
+    return jnp.where(i < half, 2 * i, 2 * (i - half) + 1)
 
 
 def kernel(
@@ -166,6 +164,8 @@
     rates[...] = rates[...] / (rows * n_ctx)
 
     header = SEGS
+    piece = seg // PARTS
+    whole = seg == rows
 
     modes = rates.shape[0]
     depth_rows = w_recv.shape[3]
@@ -273,7 +273,7 @@
             return tuple(a * s + x for a, s in zip(keep, states))
 
         zeros = tuple(jnp.zeros((SEGS, LANES), jnp.float32) for _ in range(modes))
-        last = lax.fori_loop(0, seg, first_step, zeros, unroll=4)
+        last = lax.fori_loop(0, seg, first_step, zeros, unroll=8)
         for m in range(modes):
             state[g, m] = last[m]
 
@@ -317,46 +317,60 @@
             gate[g, where, :] = gate[g, where, :] * terms[0]
             return states
 
-        lax.fori_loop(0, seg, second_step, tuple(state[g, m] for m in range(modes)), unroll=4)
-
-        @pl.loop(0, SEGS)
-        def _(s):
-            value = gate[g, pl.ds(s, seg, stride=SEGS), :]
-            sent[g, pl.ds(pl.multiple_of(s * seg, 8), seg), :] = value.astype(sent.dtype)
-
-    def out_rows(p, g):
-        return sent.at[g, pl.ds(pl.multiple_of(p * rows, 16), rows), :]
-
-    def out_copy(d, g):
+        states = tuple(state[g, m] for m in range(modes))
+        for part in range(PARTS):
+            states = lax.fori_loop(part * piece, (part + 1) * piece, second_step, states, unroll=8)
+
+            @pl.loop(0, SEGS)
+            def _(s):
+                value = gate[g, pl.ds(part * piece * SEGS + s, piece, stride=SEGS), :]
+                sent[g, pl.ds(pl.multiple_of(s * seg + part * piece, 16), piece), :] = value.astype(sent.dtype)
+
+            if whole:
+                give_out(g, part)
+        if not whole:
+            for part in range(PARTS):
+                give_out(g, part)
+
+    share = rows // PARTS
+
+    def out_rows(p, g, part):
+        return sent.at[g, pl.ds(pl.multiple_of(p * rows + part * share, 16), share), :]
+
+    def out_copy(d, g, part):
         peer = flip_traced(place, d, groups)
         return pltpu.make_async_remote_copy(
-            src_ref=out_rows(peer, g),
-            dst_ref=out.at[:, columns[g]],
-            send_sem=out_ssem.at[g, d],
-            recv_sem=out_rsem.at[g, d],
+            src_ref=out_rows(peer, g, part),
+            dst_ref=out.at[part * share : (part + 1) * share, columns[g]],
+            send_sem=out_ssem.at[g, part, d],
+            recv_sem=out_rsem.at[g, part, d],
             device_id=(team * groups + peer, ch),
             device_id_type=pl.DeviceIdType.MESH,
         )
 
-    def out_arrival(d, g):
+    def out_arrival(d, g, part):
         peer = flip_traced(place, d, groups)
-        spot = out.at[:, pl.ds(pl.multiple_of(peer * wide + g * LANES, LANES), LANES)]
+        spot = out.at[part * share : (part + 1) * share, pl.ds(pl.multiple_of(peer * wide + g * LANES, LANES), LANES)]
         return pltpu.make_async_remote_copy(
             src_ref=spot,
             dst_ref=spot,
-            send_sem=out_ssem.at[g, d],
-            recv_sem=out_rsem.at[g, d],
+            send_sem=out_ssem.at[g, part, d],
+            recv_sem=out_rsem.at[g, part, d],
             device_id=(team * groups + peer, ch),
             device_id_type=pl.DeviceIdType.MESH,
         )
 
-    own_out = [pltpu.make_async_copy(out_rows(place, g), out.at[:, columns[g]], own_sems.at[1, g]) for g in range(lane_groups)]
-    def give_out(g):
+    def own_out(g, part):
+        return pltpu.make_async_copy(
+            out_rows(place, g, part), out.at[part * share : (part + 1) * share, columns[g]], own_sems.at[1 + part, g]
+        )
+
+    def give_out(g, part):
         @pl.loop(1, groups)
         def _(d):
-            out_copy(groups - d, g).start()
-
-        own_out[g].start()
+            out_copy(groups - d, g, part).start()
+
+        own_out(g, part).start()
 
     tail = lane_groups - 1
     far = [mask for mask in masks if mask & crossing]
@@ -374,19 +388,16 @@
 
         if g < tail - 1:
             second_half(g)
-            give_out(g)
     half_way = 0
     if tail:
         project(tail, 0, half_way, in_order)
         second_half(tail - 1)
-        give_out(tail - 1)
         project(tail, half_way, chips, in_order)
     else:
         project(0, 0, chips, in_order)
     send_halo(tail)
     first_half(tail)
     second_half(tail)
-    give_out(tail)
 
     for i in range(depth):
         tok_copy(0, i).wait_send()
@@ -408,12 +419,13 @@
             def _():
                 state_copy(k, g).wait_send()
 
-        @pl.loop(1, groups)
-        def _(d):
-            out_arrival(d, g).wait_recv()
-            out_copy(d, g).wait_send()
-
-        own_out[g].wait()
+        for part in range(PARTS):
+            @pl.loop(1, groups)
+            def _(d):
+                out_arrival(d, g, part).wait_recv()
+                out_copy(d, g, part).wait_send()
+
+            own_out(g, part).wait()
 
 
 def body(n_ctx, n_ch, tokens, w_in, taps, modes_gain, decay, skip):
@@ -455,13 +467,13 @@
             dma((2**depth,)),
             dma((parts, n_ctx)),
             dma((parts, n_ctx)),
-            dma((parts, groups)),
-            dma((parts, groups)),
+            dma((parts, PARTS, groups)),
+            dma((parts, PARTS, groups)),
             dma((parts, teams)),
             dma((parts, teams)),
             dma((parts, 2)),
             dma((7,)),
-            dma((2, parts)),
+            dma((1 + PARTS, parts)),
         ],
         compiler_params=pltpu.CompilerParams(
             collective_id=0, has_side_effects=True, vmem_limit_bytes=60 * 1024 * 1024

time: 164 us -> 163 us (level)
  no operation moved by 1% of the time
where the time goes in v4:
time: 163 us
  Pallas kernels  161 us (99%)
  local copies, waits for them, and re-layouts  2.3 us (1%)
    pallas_call x1, Pallas kernels, body(): pl.pallas_call(functools.partial(kernel, n_ctx, n_ch, groups), out_shape=...  161 us

profile of v4, /device:TPU:16, one launch (start us, length us, event | category | flops | bytes accessed | tf_op | source)
XLA Modules:
  0.0 163.0 jit_solution(17683113616502542001)
XLA Ops:
  0.0 160.7 %shard_map.64 = bf16[256,2048]{1,0:T(8,128)(2,1)} custom-call(bf16[256,2048]{1,0:T(8,128)(2,1)} %tokens.1, bf16[3,256,2048]{2,1,0:T(8,128)(2,1)} %bitcast.2, f32[3,3,2048]{2,1,0:T(4,128)} %all_taps.1, f32[16,2048]{1,0:T(8,128)} %all_gains.1, f32[16,2048]{1,0:T(8,128)} %all_decay.1, f32[1,2048]{1,0:T(1,128)} %bitcast.3), custom_call_target="tpu_custom_call" | custom-call | tf_op jit(solution)/shard_map/pallas_call | solution.py:445
  160.7 2.3 %copy.8 = bf16[256,2048]{1,0:T(8,128)(2,1)} copy(bf16[256,2048]{1,0:T(8,128)(2,1)} %shard_map.64) | data formatting | bytes 2097152

commit v5 on v4

--- a/solution.py
+++ b/solution.py
@@ -38,7 +38,7 @@
 def kernel(
     n_ctx, n_ch, groups,
     tokens, w_send, all_taps, all_gains, all_decay, all_skip, out,
-    taps, gains, rates, skip, tok, w_recv, acc, prod, gate, state, ends, carry, sent, halo, halo_out,
+    taps, gains, rates, skip, tok, w_recv, acc, prod, gate, state, ends, carry, sent, halo, halo_out, coefs,
     tok_ssem, tok_rsem, w_ssem, w_rsem, out_ssem, out_rsem, st_ssem, st_rsem, halo_sems, local_sems, own_sems,
 ):
     rows, width = tokens.shape
@@ -233,8 +233,11 @@
     def row(ref, m, mine):
         return jnp.broadcast_to(ref[m : m + 1, mine], (SEGS, LANES))
 
-    def decays(mine):
-        return [jnp.exp(-row(rates, m, mine)) for m in range(modes)]
+    def prepare(g):
+        mine = slice(g * LANES, (g + 1) * LANES)
+        for m in range(modes):
+            coefs[g, 0, m] = jnp.exp(-row(rates, m, mine))
+            coefs[g, 1, m] = row(gains, m, mine) * jnp.sqrt(2.0 * row(rates, m, mine))
 
     def first_half(g):
         mine = slice(g * LANES, (g + 1) * LANES)
@@ -266,7 +269,7 @@
             gate[g, pl.ds(s, seg, stride=SEGS), :] = features[0]
             prod[g, pl.ds(s, seg, stride=SEGS), :] = features[1] * features[2]
 
-        keep = decays(mine)
+        keep = [coefs[g, 0, m] for m in range(modes)]
 
         def first_step(t, states):
             x = prod[g, pl.ds(pl.multiple_of(t * SEGS, SEGS), SEGS), :]
@@ -303,8 +306,8 @@
         for s in range(SEGS):
             state[g, :, s, :] = state[g, :, s, :] + incoming * jnp.exp(-rate * float(s * seg))
 
-        keep = decays(mine)
-        weight = [row(gains, m, mine) * jnp.sqrt(2.0 * row(rates, m, mine)) for m in range(modes)]
+        keep = [coefs[g, 0, m] for m in range(modes)]
+        weight = [coefs[g, 1, m] for m in range(modes)]
         direct = jnp.broadcast_to(skip[0:1, mine], (SEGS, LANES))
 
         def second_step(t, states):
@@ -373,6 +376,8 @@
         own_out(g, part).start()
 
     tail = lane_groups - 1
+    for g in range(lane_groups):
+        prepare(g)
     far = [mask for mask in masks if mask & crossing]
     if tail:
         project(0, 0, per_half, near_first)
@@ -463,6 +468,7 @@
             pltpu.VMEM((parts, span, LANES), jnp.bfloat16),
             pltpu.VMEM((parts, SEGS, 3 * LANES), f32),
             pltpu.VMEM((parts, SEGS, 3 * LANES), f32),
+            pltpu.VMEM((parts, 2, modes, SEGS, LANES), f32),
             dma((2**depth, depth)),
             dma((2**depth,)),
             dma((parts, n_ctx)),

time: 163 us -> 163 us (level)
  no operation moved by 1% of the time
where the time goes in v5:
time: 163 us
  Pallas kernels  161 us (99%)
  local copies, waits for them, and re-layouts  2.3 us (1%)
    pallas_call x1, Pallas kernels, body(): pl.pallas_call(functools.partial(kernel, n_ctx, n_ch, groups), out_shape=...  161 us

profile of v5, /device:TPU:16, one launch (start us, length us, event | category | flops | bytes accessed | tf_op | source)
XLA Modules:
  0.0 163.0 jit_solution(7760603328831115817)
XLA Ops:
  0.0 160.7 %shard_map.64 = bf16[256,2048]{1,0:T(8,128)(2,1)} custom-call(bf16[256,2048]{1,0:T(8,128)(2,1)} %tokens.1, bf16[3,256,2048]{2,1,0:T(8,128)(2,1)} %bitcast.2, f32[3,3,2048]{2,1,0:T(4,128)} %all_taps.1, f32[16,2048]{1,0:T(8,128)} %all_gains.1, f32[16,2048]{1,0:T(8,128)} %all_decay.1, f32[1,2048]{1,0:T(1,128)} %bitcast.3), custom_call_target="tpu_custom_call" | custom-call | tf_op jit(solution)/shard_map/pallas_call | solution.py:450
  160.7 2.3 %copy.8 = bf16[256,2048]{1,0:T(8,128)(2,1)} copy(bf16[256,2048]{1,0:T(8,128)(2,1)} %shard_map.64) | data formatting | bytes 2097152
